TPU v7x, 32 devices: a whole 2x2x4 slice. The times are simulated.
32 devices in a mesh: dp: 4 (over z), row: 4 (over y, core), col: 2 (over x).
Axes of the slice: x: 2, y: 2, z: 4, core: 2. Of those that a mesh axis runs over, the one named last changes fastest.
Arguments:
- block_input: bfloat16 [8, 1792, 1024], P('dp', None, ('row', 'col')), may hold values from -45 to 45
- segment_ids: int32 [8, 1792], P('dp'), may hold values from 0 to 3, never falling along the last dimension, each value on 1 to 896 neighbouring positions
- out_grad: bfloat16 [8, 1792, 1024], P('dp', None, ('row', 'col')), may hold values from -6 to 6
- in_weight: bfloat16 [3, 1024, 1024], P(None, 'col', 'row'), may hold values from -0.1875 to 0.1875
- out_weight: bfloat16 [1024, 1024], P('row', 'col'), may hold values from -0.375 to 0.375
- gate_weight: bfloat16 [1024, 4608], P('col', 'row'), may hold values from -0.1875 to 0.1875
- up_weight: bfloat16 [1024, 4608], P('col', 'row'), may hold values from -0.1875 to 0.1875
- down_weight: bfloat16 [4608, 1024], P('row', 'col'), may hold values from -0.1875 to 0.1875
- conv_weight: bfloat16 [3, 1024], P(None, ('row', 'col')), may hold values from -3.5 to 3.5
- mixer_norm_gain: float32 [1024], replicated, may hold values from 0.5 to 1.5
- feedforward_norm_gain: float32 [1024], replicated, may hold values from 0.5 to 1.5
Outputs:
- block_output: bfloat16 [8, 1792, 1024], P('dp', None, ('row', 'col'))
- block_input_gradient: float32 [8, 1792, 1024], P('dp', None, ('row', 'col'))
- grad_in_weight: float32 [3, 1024, 1024], P(None, 'col', 'row')
- grad_out_weight: float32 [1024, 1024], P('row', 'col')
- grad_gate_weight: float32 [1024, 4608], P('col', 'row')
- grad_up_weight: float32 [1024, 4608], P('col', 'row')
- grad_down_weight: float32 [4608, 1024], P('row', 'col')
- grad_conv_weight: float32 [3, 1024], P(None, ('row', 'col'))
- mixer_gain_gradient: float32 [1024], P(('row', 'col'))
- feedforward_gain_gradient: float32 [1024], P(('row', 'col'))
Inputs may be any that keep to these rules, and one draw needn't show every extreme that they name: `segment_ids`: along each sequence the segment numbers never fall; a segment covers at most half of 1792 positions.
All inputs are finite; a program needn't handle non-finite values.
Results may differ from a plain program's by a relative error of at most 0.013.
Values may be sent and summed in bfloat16 or wider, within the bound.
No kernel may reach another device: no remote copies, remote signals or barrier semaphores. Data moves between devices by JAX's collectives and lax.ppermute only.
A program may use at most 256 MiB of HBM per device.

v0:
```python
import jax
import jax.numpy as jnp
from jax import lax
from jax.sharding import PartitionSpec as P

D = 1024
EPS = 1e-05


def lagged(values, shift_by):
    padding = jnp.zeros_like(values[..., :shift_by, :])
    return jnp.concatenate([padding, values[..., :-shift_by, :]], axis=-2)


def leading(values, shift_by):
    padding = jnp.zeros_like(values[..., :shift_by, :])
    return jnp.concatenate([values[..., shift_by:, :], padding], axis=-2)


def same_masks(segments):
    mask_list = []
    for shift_by in (1, 2):
        filler = jnp.full(segments[..., :shift_by].shape, -1, jnp.int32)
        earlier = jnp.concatenate([filler, segments[..., :-shift_by]], axis=-1)
        mask_list.append(jnp.where(earlier == segments, 1.0, 0.0).astype(jnp.float32)[..., None])
    return mask_list


def conv_forward(mixed_in, mask_list, kernel):
    return (
        kernel[0] * mixed_in
        + kernel[1] * mask_list[0] * lagged(mixed_in, 1)
        + kernel[2] * mask_list[1] * lagged(mixed_in, 2)
    )


def conv_backward(d_conved, mixed_in, mask_list, kernel):
    first_term = mask_list[0] * d_conved
    second = mask_list[1] * d_conved
    d_mixed = (
        kernel[0] * d_conved + kernel[1] * leading(first_term, 1) + kernel[2] * leading(second, 2)
    )
    all_axes = tuple(range(d_conved.ndim - 1))
    d_kernel = jnp.stack(
        [
            jnp.sum(d_conved * mixed_in, axis=all_axes),
            jnp.sum(first_term * lagged(mixed_in, 1), axis=all_axes),
            jnp.sum(second * lagged(mixed_in, 2), axis=all_axes),
        ]
    )
    return (d_mixed, d_kernel)


def full_width(part_half):
    return lax.all_gather(part_half, ("row", "col"), axis=1, tiled=True)


def own_share(partial_sum):
    return lax.psum_scatter(partial_sum, ("row", "col"), scatter_dimension=1, tiled=True)


def summed_all(partial_sum):
    return lax.psum(partial_sum, ("row", "col"))


def token_stat(values):
    return lax.psum(jnp.sum(values, axis=1), ("row", "col"))


def full_scale(values):
    return lax.rsqrt(jnp.mean(values * values, axis=1, keepdims=True) + EPS)


def norm_reverse_result(d_normed, x_hat, scale_row, gain_row):
    d_hat = d_normed * gain_row
    mean_term = token_stat(d_hat * x_hat)[:, None] / D
    return scale_row * (d_hat - x_hat * mean_term)


def body(
    block_input,
    segment_ids,
    out_grad,
    in_weight,
    out_weight,
    gate_weight,
    up_weight,
    down_weight,
    conv_weight,
    mixer_norm_gain,
    feedforward_norm_gain,
):
    seq_count, seq_length, own_width = block_input.shape
    tok_rows = seq_count * seq_length
    own_start = (lax.axis_index("row") * lax.axis_size("col") + lax.axis_index("col")) * own_width
    kernel = conv_weight.astype(jnp.float32)
    local_mixer_gain = lax.dynamic_slice_in_dim(mixer_norm_gain, own_start, own_width)
    local_feedforward_gain = lax.dynamic_slice_in_dim(feedforward_norm_gain, own_start, own_width)
    input_half = block_input.reshape(tok_rows, own_width)
    local_input = input_half.astype(jnp.float32)
    upstream_gradient = out_grad.reshape(tok_rows, own_width)
    mask_list = same_masks(segment_ids)
    mixer_in, mixer_out = (
        lax.all_to_all(in_weight, "col", split_axis=2, concat_axis=1, tiled=True),
        lax.all_to_all(
            jnp.transpose(out_weight)[None], "col", split_axis=2, concat_axis=1, tiled=True
        ),
    )
    mixer_out = mixer_out[0]
    swiglu_gate, swiglu_up, swiglu_down = (
        lax.all_to_all(gate_weight, "col", split_axis=1, concat_axis=0, tiled=True),
        lax.all_to_all(up_weight, "col", split_axis=1, concat_axis=0, tiled=True),
        lax.all_to_all(jnp.transpose(down_weight), "col", split_axis=1, concat_axis=0, tiled=True),
    )
    complete_input = full_width(input_half).astype(jnp.float32)
    mixer_inverse_scale = full_scale(complete_input)
    mixer_normed = (complete_input * mixer_inverse_scale * mixer_norm_gain).astype(jnp.bfloat16)
    mixer_normalized = local_input * mixer_inverse_scale
    projected = jnp.einsum(
        "td,jdc->jtc", mixer_normed, mixer_in, preferred_element_type=jnp.float32
    )
    shaped = projected.reshape(3, seq_count, seq_length, own_width)
    b_proj, c_proj, x_proj = (shaped[0], shaped[1], shaped[2])
    mixed_in = b_proj * x_proj
    conved = conv_forward(mixed_in, mask_list, kernel)
    gated_out = (c_proj * conved).astype(jnp.bfloat16).reshape(tok_rows, own_width)
    mixer_partial = jnp.einsum(
        "tc,dc->td", gated_out, mixer_out, preferred_element_type=jnp.float32
    )
    resid_full = complete_input + summed_all(mixer_partial)
    feedforward_inverse_scale = full_scale(resid_full)
    feedforward_normed = (resid_full * feedforward_inverse_scale * feedforward_norm_gain).astype(
        jnp.bfloat16
    )
    local_residual = lax.dynamic_slice_in_dim(resid_full, own_start, own_width, axis=1)
    feedforward_normalized = local_residual * feedforward_inverse_scale
    gate_pre = jnp.dot(feedforward_normed, swiglu_gate, preferred_element_type=jnp.float32)
    up_pre = jnp.dot(feedforward_normed, swiglu_up, preferred_element_type=jnp.float32)
    sigmoid = jax.nn.sigmoid(gate_pre)
    activated = (gate_pre * sigmoid * up_pre).astype(jnp.bfloat16)
    swiglu_partial = jnp.einsum(
        "tf,df->td", activated, swiglu_down, preferred_element_type=jnp.float32
    )
    swiglu_full = summed_all(swiglu_partial)
    output_own = local_residual + lax.dynamic_slice_in_dim(
        swiglu_full, own_start, own_width, axis=1
    )
    cot_full = full_width(upstream_gradient)
    d_act = jnp.einsum("td,df->tf", cot_full, swiglu_down, preferred_element_type=jnp.float32)
    grad_down_piece = jnp.einsum(
        "td,tf->df", cot_full, activated, preferred_element_type=jnp.float32
    )
    d_up = (d_act * gate_pre * sigmoid).astype(jnp.bfloat16)
    d_gate = (d_act * up_pre * sigmoid * (1.0 + gate_pre * (1.0 - sigmoid))).astype(jnp.bfloat16)
    grad_gate_piece = jnp.einsum(
        "td,tf->df", feedforward_normed, d_gate, preferred_element_type=jnp.float32
    )
    grad_up_piece = jnp.einsum(
        "td,tf->df", feedforward_normed, d_up, preferred_element_type=jnp.float32
    )
    norm_two_partial = jnp.einsum(
        "tf,df->td", d_gate, swiglu_gate, preferred_element_type=jnp.float32
    ) + jnp.einsum("tf,df->td", d_up, swiglu_up, preferred_element_type=jnp.float32)
    grad_gate_w, grad_up_w, grad_down_t = (
        lax.all_to_all(
            grad_gate_piece.astype(jnp.bfloat16), "col", split_axis=0, concat_axis=1, tiled=True
        ).astype(grad_gate_piece.dtype),
        lax.all_to_all(
            grad_up_piece.astype(jnp.bfloat16), "col", split_axis=0, concat_axis=1, tiled=True
        ).astype(grad_up_piece.dtype),
        lax.all_to_all(
            grad_down_piece.astype(jnp.bfloat16), "col", split_axis=0, concat_axis=1, tiled=True
        ).astype(grad_down_piece.dtype),
    )
    grad_down_w = jnp.transpose(grad_down_t)
    feedforward_normed_gradient = own_share(norm_two_partial)
    feedforward_gain_gradient = jnp.sum(
        feedforward_normed_gradient * feedforward_normalized, axis=0
    )
    residual_gradient = upstream_gradient.astype(jnp.float32) + norm_reverse_result(
        feedforward_normed_gradient,
        feedforward_normalized,
        feedforward_inverse_scale,
        local_feedforward_gain,
    )
    resid_grad_full = full_width(residual_gradient.astype(jnp.bfloat16))
    grad_out_piece = jnp.einsum(
        "td,tc->dc", resid_grad_full, gated_out, preferred_element_type=jnp.float32
    )
    d_gated = jnp.einsum(
        "td,dc->tc", resid_grad_full, mixer_out, preferred_element_type=jnp.float32
    )
    d_gated = d_gated.reshape(seq_count, seq_length, own_width)
    d_cproj = (d_gated * conved).astype(jnp.bfloat16)
    d_conved = d_gated * c_proj
    d_mixed, grad_kernel = conv_backward(d_conved, mixed_in, mask_list, kernel)
    d_bproj = (d_mixed * x_proj).astype(jnp.bfloat16)
    d_xproj = (d_mixed * b_proj).astype(jnp.bfloat16)
    d_projected = jnp.stack([d_bproj, d_cproj, d_xproj]).reshape(3, tok_rows, own_width)
    grad_in_piece = jnp.einsum(
        "td,jtc->jdc", mixer_normed, d_projected, preferred_element_type=jnp.float32
    )
    norm_one_partial = jnp.einsum(
        "jtc,jdc->td", d_projected, mixer_in, preferred_element_type=jnp.float32
    )
    grad_in_w, grad_out_t = (
        lax.all_to_all(
            grad_in_piece.astype(jnp.bfloat16), "col", split_axis=1, concat_axis=2, tiled=True
        ).astype(grad_in_piece.dtype),
        lax.all_to_all(
            grad_out_piece[None].astype(jnp.bfloat16),
            "col",
            split_axis=1,
            concat_axis=2,
            tiled=True,
        ).astype(jnp.float32),
    )
    grad_out_w = jnp.transpose(grad_out_t[0])
    mixer_normed_gradient = own_share(norm_one_partial)
    mixer_gain_gradient = jnp.sum(mixer_normed_gradient * mixer_normalized, axis=0)
    block_input_gradient = residual_gradient + norm_reverse_result(
        mixer_normed_gradient, mixer_normalized, mixer_inverse_scale, local_mixer_gain
    )
    (
        in_total,
        out_total,
        gate_total,
        up_total,
        down_total,
        kernel_total,
        gain_one_total,
        gain_two_total,
    ) = (
        lax.psum(grad_in_w.astype(jnp.bfloat16), "dp").astype(jnp.float32),
        lax.psum(grad_out_w.astype(jnp.bfloat16), "dp").astype(jnp.float32),
        lax.psum(grad_gate_w.astype(jnp.bfloat16), "dp").astype(jnp.float32),
        lax.psum(grad_up_w.astype(jnp.bfloat16), "dp").astype(jnp.float32),
        lax.psum(grad_down_w.astype(jnp.bfloat16), "dp").astype(jnp.float32),
        lax.psum(grad_kernel.astype(jnp.bfloat16), "dp").astype(jnp.float32),
        lax.psum(mixer_gain_gradient.astype(jnp.bfloat16), "dp").astype(jnp.float32),
        lax.psum(feedforward_gain_gradient.astype(jnp.bfloat16), "dp").astype(jnp.float32),
    )
    block_output = output_own.astype(jnp.bfloat16).reshape(seq_count, seq_length, own_width)
    return (
        block_output,
        block_input_gradient.reshape(seq_count, seq_length, own_width),
        in_total,
        out_total,
        gate_total,
        up_total,
        down_total,
        kernel_total,
        gain_one_total,
        gain_two_total,
    )


def solution(mesh):
    placed = (
        P("dp", None, ("row", "col")),
        P("dp", None),
        P("dp", None, ("row", "col")),
        P(None, "col", "row"),
        P("row", "col"),
        P("col", "row"),
        P("col", "row"),
        P("row", "col"),
        P(None, ("row", "col")),
        P(),
        P(),
    )
    return jax.shard_map(
        body,
        mesh=mesh,
        in_specs=placed,
        out_specs=(
            P("dp", None, ("row", "col")),
            P("dp", None, ("row", "col")),
            P(None, "col", "row"),
            P("row", "col"),
            P("col", "row"),
            P("col", "row"),
            P("row", "col"),
            P(None, ("row", "col")),
            P(("row", "col")),
            P(("row", "col")),
        ),
        check_vma=False,
    )
```

profile of v0, /device:TPU:0, one launch (start us, length us, event | category | flops | bytes accessed | tf_op | source)
XLA Modules:
  0.0 1171.5 jit_solution(15314142527145957673)
XLA Ops:
  10.0 2.2 reduce
  13.1 4.2 all-to-all-start.1
  17.3 1.7 copy.81
  19.1 4.5 all-to-all-done.1
  23.6 3.6 all-to-all-start
  28.1 16.2 %all-to-all-done = bf16[3,512,256]{1,0,2:T(4,128)(2,1)S(1)} async-done(((bf16[3,512,256]{1,0,2:T(4,128)(2,1)}), bf16[3,512,256]{1,0,2:T(4,128)(2,1)S(1)}, u32[]{:S(2)}, u32[]{:S(2)}) %all-to-all-start) | async-done | bytes 786464 | tf_op jit(solution)/shard_map/all_to_all | solution.py:104
  45.1 22.4 %all-gather.4.cloned.1.call-done = bf16[3584,1024]{1,0:T(8,128)(2,1)} async-done(((bf16[3584,128]{1,0:T(8,128)(2,1)}), bf16[3584,1024]{1,0:T(8,128)(2,1)}) %all-gather.4.cloned.1.call-update) | async-done | bytes 7340048 | tf_op jit(solution)/shard_map/all_gather | solution.py:55
  67.5 4.7 fusion
  72.7 4.0 convolution_bitcast_fusion.1
  79.5 2.5 multiply_convert_fusion.7
  83.0 7.3 fusion.18
  93.0 3.7 all-to-all-start.2
  96.7 2.4 copy.88
  99.2 26.4 %all-to-all-done.2 = bf16[512,2,576]{0,2,1:T(8,128)(2,1)S(1)} async-done(((bf16[512,2,576]{0,2,1:T(8,128)(2,1)}), bf16[512,2,576]{0,2,1:T(8,128)(2,1)S(1)}, u32[]{:S(2)}, u32[]{:S(2)}) %all-to-all-start.2) | async-done | bytes 1179680 | tf_op jit(solution)/shard_map/all_to_all | solution.py:111
  125.6 33.1 %all_to_all.168 = bf16[512,2,576]{0,2,1:T(8,128)(2,1)} all-to-all(bf16[512,2,576]{0,2,1:T(8,128)(2,1)} %bitcast.166), channel_id=1, replica_groups=mesh['dp'=4,'row'=4,'col'=2] {'col'}, dimensions={1} | all-to-all | bytes 2359296 | tf_op jit(solution)/shard_map/all_to_all | solution.py:112
  158.7 4.5 all-to-all-start.4
  166.3 25.3 %all-to-all-done.4 = bf16[512,2,576]{0,2,1:T(8,128)(2,1)} async-done(((bf16[512,2,576]{0,2,1:T(8,128)(2,1)}), bf16[512,2,576]{0,2,1:T(8,128)(2,1)}, u32[]{:S(2)}, u32[]{:S(2)}) %all-to-all-start.4) | async-done | bytes 1179680 | tf_op jit(solution)/shard_map/all_to_all | solution.py:113
  191.6 1.4 copy.109
  193.1 130.1 %all-reduce.12.cloned.1.call-done = f32[3584,1024]{1,0:T(8,128)} async-done(((f32[3584,1024]{1,0:T(8,128)}), f32[3584,1024]{1,0:T(8,128)}) %all-reduce.12.cloned.1.call-update) | async-done | bytes 14680080 | tf_op jit(solution)/shard_map/psum | solution.py:63
  323.2 13.8 %multiply_reduce_fusion = (f32[3584]{0:T(1024)S(1)}, f32[3584,1024]{1,0:T(8,128)}) fusion(f32[3584,1024]{1,0:T(8,128)} %all-reduce.12.cloned.1.call-done, bf16[3584,1024]{1,0:T(8,128)(2,1)} %all-gather.4.cloned.1.call-done), kind=kLoop, calls=%fused_computation.7 | loop fusion | flops 14676480 | bytes 36714496 | tf_op jit(solution)/shard_map/reduce_sum | solution.py:71
  337.0 9.4 multiply_convert_fusion
  346.4 11.2 fusion.19
  357.6 6.7 fusion.20
  364.3 12.2 %all-gather.6.cloned.1.call-done = bf16[3584,1024]{1,0:T(8,128)(2,1)} async-done(((bf16[3584,128]{1,0:T(8,128)(2,1)}), bf16[3584,1024]{1,0:T(8,128)(2,1)}) %all-gather.6.cloned.1.call-update) | async-done | bytes 7340048 | tf_op jit(solution)/shard_map/all_gather | solution.py:55
  376.5 15.9 %multiply_convert_fusion.1 = (bf16[3584,576]{0,1:T(8,128)(2,1)S(1)}, bf16[3584,576]{0,1:T(8,128)(2,1)S(1)}, bf16[3584,576]{0,1:T(8,128)(2,1)}) fusion(f32[3584,576]{0,1:T(8,128)} %fusion.19, f32[3584,576]{0,1:T(8,128)} %fusion.20, bf16[3584,1024]{1,0:T(8,128)(2,1)} %all-gather.6.cloned.1.call-done, bf16[1024,576]{0,1:T(8,128)(2,1)S(1)} %bitcast.187), kind=kOutput, calls=%fused_computation.9 | convolution fusion | flops 4260888576 | bytes 37421056 | tf_op jit(solution)/shard_map/td,df->tf/dot_general | solution.py:149
  392.4 9.6 fusion.22
  402.0 12.3 %convolution_add_fusion = f32[3584,1024]{1,0:T(8,128)} fusion(f32[3584,1024]{1,0:T(8,128)} %fusion.22, bf16[3584,576]{0,1:T(8,128)(2,1)S(1)} %get-tuple-element.74, bf16[1024,576]{0,1:T(8,128)(2,1)S(1)} %bitcast.192), kind=kOutput, calls=%fused_computation.13 | convolution fusion | flops 4231528448 | bytes 34668544 | tf_op jit(solution)/shard_map/tf,df->td/dot_general | solution.py:163
  414.4 102.2 %reduce-scatter.3.cloned.1.call-done = f32[3584,128]{1,0:T(8,128)} async-done(((f32[3584,1024]{1,0:T(8,128)}), f32[3584,128]{1,0:T(8,128)}) %reduce-scatter.3.cloned.1.call-update) | async-done | bytes 1835024 | tf_op jit(solution)/shard_map/reduce_scatter | solution.py:59
  516.6 4.1 multiply_reduce_fusion.1
  520.7 23.8 %psum.86 = f32[3584]{0:T(1024)S(1)} all-reduce(f32[3584]{0:T(1024)S(1)} %get-tuple-element.51), channel_id=1, replica_groups=mesh['dp'=4,'row'=4,'col'=2] {'row','col'}, use_global_device_ids=true, to_apply=%region_6.7 | all-reduce | flops 3584 | bytes 28672 | tf_op jit(solution)/shard_map/psum | solution.py:67
  544.6 4.3 fusion.16
  548.9 8.8 convolution_convert_fusion.1
  558.7 3.8 all-to-all-start.7
  562.5 8.8 convolution_convert_fusion
  572.4 32.6 %all-gather.8.cloned.1.call-done = bf16[3584,1024]{1,0:T(8,128)(2,1)} async-done(((bf16[3584,128]{1,0:T(8,128)(2,1)}), bf16[3584,1024]{1,0:T(8,128)(2,1)}) %all-gather.8.cloned.1.call-update) | async-done | bytes 7340048 | tf_op jit(solution)/shard_map/all_gather | solution.py:55
  605.1 7.8 multiply_reduce_fusion.5
  612.8 1.9 multiply_reduce_fusion.4
  616.3 2.0 multiply_convert_fusion.6
  618.3 4.6 all-to-all-start.8
  623.0 5.2 fusion.13
  628.6 2.3 reduce.1
  631.7 2.7 multiply_convert_fusion.4
  634.4 4.3 all-to-all-done.8
  638.7 3.7 all-to-all-start.6
  642.4 6.9 fusion.10
  650.8 3.6 all-to-all-start.5
  654.4 8.8 convolution_convert_fusion.2
  664.2 3.6 all-to-all-done.5
  667.8 3.6 all-to-all-start.9
  674.4 1.8 copy.93
  676.2 3.1 all_to_all.146
  679.3 6.1 all-to-all-done.9
  687.0 10.6 convolution_bitcast_fusion
  698.9 11.3 fusion.21
  711.4 142.0 %all-reduce.16.cloned.1.call-done = (bf16[512,1152]{0,1:T(8,128)(2,1)}, bf16[512,1152]{0,1:T(8,128)(2,1)}, bf16[3,512,256]{2,1,0:T(8,128)(2,1)}, bf16[256,512]{1,0:T(8,128)(2,1)}, bf16[1152,512]{1,0:T(8,128)(2,1)}) async-done(((bf16[512,1152]{0,1:T(8,128)(2,1)}, bf16[512,1152]{0,1:T(8,128)(2,1)}, bf16[3,512,256]{2,1,0:T(8,128)(2,1)}, bf16[256,512]{1,0:T(8,128)(2,1)}, bf16[1152,512]{1,0:T(8,128)(2,1)}), ...) | async-done | bytes 4587536 | tf_op jit(solution)/shard_map/psum | solution.py:236
  853.4 3.1 convert_element_type.173
  856.6 1.7 copy.100
  858.3 1.7 copy.99
  862.2 95.9 %reduce-scatter.5.cloned.1.call-done = f32[3584,128]{1,0:T(8,128)} async-done(((f32[3584,1024]{1,0:T(8,128)}), f32[3584,128]{1,0:T(8,128)}) %reduce-scatter.5.cloned.1.call-update) | async-done | bytes 1835024 | tf_op jit(solution)/shard_map/reduce_scatter | solution.py:59
  958.1 3.0 multiply_reduce_fusion.2
  961.1 11.7 all-reduce.6
  974.5 25.8 %psum.87 = f32[3584]{0:T(1024)S(1)} all-reduce(f32[3584]{0:T(1024)S(1)} %get-tuple-element.53), channel_id=1, replica_groups=mesh['dp'=4,'row'=4,'col'=2] {'row','col'}, use_global_device_ids=true, to_apply=%region_9.10 | all-reduce | flops 3584 | bytes 28672 | tf_op jit(solution)/shard_map/psum | solution.py:67
  1000.2 157.4 %all-reduce.14.cloned.1.call-done = f32[3584,1024]{1,0:T(8,128)} async-done(((f32[3584,1024]{1,0:T(8,128)}), f32[3584,1024]{1,0:T(8,128)}) %all-reduce.14.cloned.1.call-update) | async-done | bytes 14680080 | tf_op jit(solution)/shard_map/psum | solution.py:63
  1157.6 6.7 multiply_add_fusion
  (155 shorter events, 33.8 us)
Async XLA Ops:
  7.2 60.3 %all-gather.4.cloned.1.call-start = ((), (), s32[]{:S(2)}) async-start(), calls=%async_computation.12 | async-start | bytes 8257536 | tf_op jit(solution)/shard_map/all_gather | solution.py:55
  7.2 10.1 copy-start.26
  10.0 9.1 copy-start.44
  13.1 10.5 all-to-all-start.1
  17.3 10.1 copy-start.34
  23.6 20.7 %all-to-all-start = ((bf16[3,512,256]{1,0,2:T(4,128)(2,1)}), bf16[3,512,256]{1,0,2:T(4,128)(2,1)S(1)}, u32[]{:S(2)}, u32[]{:S(2)}) async-start(bf16[3,512,256]{1,0,2:T(4,128)(2,1)} %copy.81), calls=%async_computation | async-start | bytes 2097152 | tf_op jit(solution)/shard_map/all_to_all | solution.py:104
  27.2 296.0 %all-reduce.12.cloned.1.call-start = ((), (), s32[]{:S(2)}) async-start(), calls=%async_computation.13 | async-start | bytes 29360128 | tf_op jit(solution)/shard_map/psum | solution.py:63
  45.1 27.2 %copy-start.17 = (bf16[3,512,2,128]{3,1,2,0:T(8,128)(2,1)}, bf16[3,512,2,128]{3,1,2,0:T(8,128)(2,1)S(1)}, u32[]{:S(2)}) copy-start(bf16[3,512,2,128]{3,1,2,0:T(8,128)(2,1)S(1)} %copy.82) | copy-start | bytes 2359300
  45.1 27.2 %copy-start.45 = (f32[1024]{0:T(1024)S(1)}, f32[1024]{0:T(1024)}, u32[]{:S(2)}) copy-start(f32[1024]{0:T(1024)} %param.20) | copy-start | bytes 12292
  67.5 5.2 copy-start
  72.3 4.5 copy-start.29
  77.1 1.2 copy-start.3
  77.1 1.8 copy-start.5
  77.1 2.4 copy-start.2
  82.1 0.9 copy-start.13
  90.3 1.3 copy-start.20
  90.3 286.1 %all-gather.6.cloned.1.call-start = ((), (), s32[]{:S(2)}) async-start(), calls=%async_computation.15 | async-start | bytes 8257536 | tf_op jit(solution)/shard_map/all_gather | solution.py:55
  93.0 32.6 %all-to-all-start.2 = ((bf16[512,2,576]{0,2,1:T(8,128)(2,1)}), bf16[512,2,576]{0,2,1:T(8,128)(2,1)S(1)}, u32[]{:S(2)}, u32[]{:S(2)}) async-start(bf16[512,2,576]{0,2,1:T(8,128)(2,1)} %bitcast.165), calls=%async_computation.2 | async-start | bytes 2359296 | tf_op jit(solution)/shard_map/all_to_all | solution.py:111
  158.7 33.0 %all-to-all-start.4 = ((bf16[512,2,576]{0,2,1:T(8,128)(2,1)}), bf16[512,2,576]{0,2,1:T(8,128)(2,1)}, u32[]{:S(2)}, u32[]{:S(2)}) async-start(bf16[512,2,576]{0,2,1:T(8,128)(2,1)} %bitcast.186), calls=%async_computation.4 | async-start | bytes 2359296 | tf_op jit(solution)/shard_map/all_to_all | solution.py:113
  163.1 353.5 %reduce-scatter.3.cloned.1.call-start = ((), (), s32[]{:S(2)}) async-start(), calls=%async_computation.16 | async-start | bytes 16515072 | tf_op jit(solution)/shard_map/reduce_scatter | solution.py:59
  163.4 1.7 copy-start.12
  193.0 183.4 %copy-start.21 = (bf16[2,72,8,512]{3,2,0,1:T(8,128)(2,1)}, bf16[2,72,8,512]{3,2,0,1:T(8,128)(2,1)S(1)}, u32[]{:S(2)}) copy-start(bf16[2,72,8,512]{3,2,0,1:T(8,128)(2,1)S(1)} %copy.109) | copy-start | bytes 3538948
  193.1 143.9 %copy-start.38 = (f32[1024]{0:T(1024)S(1)}, f32[1024]{0:T(1024)}, u32[]{:S(2)}) copy-start(f32[1024]{0:T(1024)} %param.21) | copy-start | bytes 12292
  346.4 11.2 copy-start.9
  346.4 11.2 copy-start.24
  376.5 15.9 %copy-start.23 = (bf16[2,72,8,512]{3,2,0,1:T(8,128)(2,1)S(1)}, bf16[2,72,8,512]{3,2,0,1:T(8,128)(2,1)}, u32[]{:S(2)}) copy-start(bf16[2,72,8,512]{3,2,0,1:T(8,128)(2,1)} %copy.107) | copy-start | bytes 3538948
  392.4 9.6 copy-start.48
  392.4 9.6 copy-start.47
  392.4 9.6 copy-start.25
  414.3 190.8 %all-gather.8.cloned.1.call-start = ((), (), s32[]{:S(2)}) async-start(), calls=%async_computation.17 | async-start | bytes 8257536 | tf_op jit(solution)/shard_map/all_gather | solution.py:55
  414.4 130.1 %copy-start.35 = (f32[128]{0:T(128)}, f32[128]{0:T(128)S(1)}, u32[]{:S(2)}) copy-start(f32[128]{0:T(128)S(1)} %dynamic_slice.14) | copy-start | bytes 1540
  414.4 130.1 %copy-start.8 = (bf16[2,1792,128]{2,1,0:T(8,128)(2,1)S(1)}, bf16[2,1792,128]{2,1,0:T(8,128)(2,1)}, u32[]{:S(2)}) copy-start(bf16[2,1792,128]{2,1,0:T(8,128)(2,1)} %param.13) | copy-start | bytes 2752516
  544.5 4.3 copy-start.32
  558.7 59.6 %all-to-all-start.7 = ((bf16[2,512,576]{1,2,0:T(8,128)(2,1)}), bf16[2,512,576]{1,2,0:T(8,128)(2,1)S(1)}, u32[]{:S(2)}, u32[]{:S(2)}) async-start(bf16[2,512,576]{1,2,0:T(8,128)(2,1)} %bitcast.162), calls=%async_computation.9 | async-start | bytes 2359296 | tf_op jit(solution)/shard_map/all_to_all | solution.py:165
  614.8 1.5 copy-start.6
  618.3 4.6 copy-start.14
  618.3 9.8 copy-start.10
  618.3 20.4 %all-to-all-start.8 = ((bf16[2,512,576]{1,2,0:T(8,128)(2,1)}), bf16[2,512,576]{1,2,0:T(8,128)(2,1)}, u32[]{:S(2)}, u32[]{:S(2)}) async-start(bf16[2,512,576]{1,2,0:T(8,128)(2,1)} %bitcast.140), calls=%async_computation.10 | async-start | bytes 2359296 | tf_op jit(solution)/shard_map/all_to_all | solution.py:168
  628.2 3.5 copy-start.4
  631.7 10.7 copy-start.15
  631.7 10.7 copy-start.30
  631.7 10.7 copy-start.46
  638.7 12.0 %all-to-all-start.6 = ((bf16[2,2,32768]{2,1,0:T(2,128)(2,1)}), bf16[2,2,32768]{2,1,0:T(2,128)(2,1)S(1)}, u32[]{:S(2)}, u32[]{:S(2)}) async-start(bf16[2,2,32768]{2,1,0:T(2,128)(2,1)} %reshape.120), calls=%async_computation.8 | async-start | bytes 524288 | tf_op jit(solution)/shard_map/all_to_all | solution.py:210
  650.8 17.0 %all-to-all-start.5 = ((bf16[3,1024,128]{2,0,1:T(4,128)(2,1)}), bf16[3,1024,128]{2,0,1:T(4,128)(2,1)S(1)}, u32[]{:S(2)}, u32[]{:S(2)}) async-start(bf16[3,1024,128]{2,0,1:T(4,128)(2,1)} %copy.92), calls=%async_computation.7 | async-start | bytes 2097152 | tf_op jit(solution)/shard_map/all_to_all | solution.py:207
  667.8 17.6 %all-to-all-start.9 = ((bf16[2,512,576]{1,2,0:T(8,128)(2,1)}), bf16[2,512,576]{1,2,0:T(8,128)(2,1)S(1)}, u32[]{:S(2)}, u32[]{:S(2)}) async-start(bf16[2,512,576]{1,2,0:T(8,128)(2,1)} %bitcast.139), calls=%async_computation.11 | async-start | bytes 2359296 | tf_op jit(solution)/shard_map/all_to_all | solution.py:171
  671.4 182.0 %all-reduce.16.cloned.1.call-start = ((), (), s32[]{:S(2)}) async-start(), calls=%async_computation.19 | async-start | bytes 9175040 | tf_op jit(solution)/shard_map/psum | solution.py:236
  685.4 1.0 copy-start.11
  685.4 1.6 copy-start.16
  686.4 271.7 %reduce-scatter.5.cloned.1.call-start = ((), (), s32[]{:S(2)}) async-start(), calls=%async_computation.18 | async-start | bytes 16515072 | tf_op jit(solution)/shard_map/reduce_scatter | solution.py:59
  697.6 1.3 copy-start.22
  697.6 460.0 %all-reduce.14.cloned.1.call-start = ((), (), s32[]{:S(2)}) async-start(), calls=%async_computation.14 | async-start | bytes 29360128 | tf_op jit(solution)/shard_map/psum | solution.py:63
  710.2 0.7 copy-start.42
  853.4 3.1 copy-start.19
  856.5 1.7 copy-start.18
  858.3 1.7 copy-start.27
  860.0 1.3 copy-start.28
  860.0 98.1 %copy-start.7 = (bf16[2,1792,128]{2,1,0:T(8,128)(2,1)S(1)}, bf16[2,1792,128]{2,1,0:T(8,128)(2,1)}, u32[]{:S(2)}) copy-start(bf16[2,1792,128]{2,1,0:T(8,128)(2,1)} %param.11) | copy-start | bytes 2752516
  861.3 99.8 %copy-start.37 = (bf16[3,128]{1,0:T(4,128)(2,1)S(1)}, bf16[3,128]{1,0:T(4,128)(2,1)}, u32[]{:S(2)}) copy-start(bf16[3,128]{1,0:T(4,128)(2,1)} %pad_maximum_fusion.3) | copy-start | bytes 2308
  861.3 99.8 %copy-start.43 = (bf16[128]{0:T(256)(128)(2,1)S(1)}, bf16[128]{0:T(256)(128)(2,1)}, u32[]{:S(2)}) copy-start(bf16[128]{0:T(256)(128)(2,1)} %get-tuple-element.50) | copy-start | bytes 772
  861.3 296.3 %copy-start.1 = (f32[3584,128]{1,0:T(8,128)S(1)}, f32[3584,128]{1,0:T(8,128)}, u32[]{:S(2)}) copy-start(f32[3584,128]{1,0:T(8,128)} %reduce-scatter.3.cloned.1.call-done) | copy-start | bytes 5505028
  861.3 296.3 %copy-start.31 = (f32[3584]{0:T(1024)S(1)}, f32[3584]{0:T(1024)}, u32[]{:S(2)}) copy-start(f32[3584]{0:T(1024)} %copy-done.29) | copy-start | bytes 43012
  861.3 296.3 %copy-start.33 = (f32[3584]{0:T(1024)S(1)}, f32[3584]{0:T(1024)}, u32[]{:S(2)}) copy-start(f32[3584]{0:T(1024)} %copy-done.32) | copy-start | bytes 43012
  861.3 296.3 %copy-start.36 = (f32[128]{0:T(128)S(1)}, f32[128]{0:T(128)}, u32[]{:S(2)}) copy-start(f32[128]{0:T(128)} %copy-done.35) | copy-start | bytes 1540
  861.3 296.3 %copy-start.40 = (f32[128]{0:T(128)S(1)}, f32[128]{0:T(128)}, u32[]{:S(2)}) copy-start(f32[128]{0:T(128)} %dynamic_slice.15) | copy-start | bytes 1540
  (2 other events, 1.3 us)
Sparse Core Ops, SparseCore 0:
  9.9 57.6 all-gather.3
  90.4 232.7 all-reduce.11
  325.1 51.3 all-gather.5
  414.4 102.1 reduce-scatter.2
  549.0 56.0 all-gather.7
  686.5 166.8 all-reduce.15
  856.9 101.1 reduce-scatter.4
  961.6 196.0 all-reduce.13
where the time goes:
time: 1180 us; the launch traced here: 1170 us
  waiting for transfers between devices  783 us (66%)
  matrix products  135 us (11%)
  blocking collectives  94.4 us (8%)
  other arithmetic  67.4 us (6%)
  local copies, waits for them, and re-layouts  40.8 us (3%)
  starting transfers between devices  36.2 us (3%)
  between operations  15 us (1%)
    psum x2, waiting for transfers between devices, summed_all(): return lax.psum(partial_sum, ('row', 'col'))  288 us
    reduce_scatter x2, waiting for transfers between devices, own_share(): lax.psum_scatter(partial_sum, ('row', 'col'), scatter_dimension=1, tiled=...  198 us
    psum x1, waiting for transfers between devices, body(): lax.psum(grad_gate_w.astype(jnp.bfloat16), 'dp').astype(jnp.float32)  142 us
    all_gather x3, waiting for transfers between devices, full_width(): return lax.all_gather(part_half, ('row', 'col'), axis=1, tiled=True)  67.3 us
    psum x2, blocking collectives, token_stat(): return lax.psum(jnp.sum(values, axis=1), ('row', 'col'))  49.6 us
    all_to_all x1, blocking collectives, body(): lax.all_to_all(up_weight, 'col', split_axis=1, concat_axis=0, tiled=True)  33.1 us
    all_to_all x1, waiting for transfers between devices, body(): lax.all_to_all(gate_weight, 'col', split_axis=1, concat_axis=0, tiled=True)  26.4 us
    all_to_all x1, waiting for transfers between devices, body(): lax.all_to_all(jnp.transpose(down_weight), 'col', split_axis=1, concat_ax...  25.3 us
  transfers between devices with their start and end apart: 17, of which 15 were waited for; matrix products, arithmetic and copies ran while one was open for 14% of the time, Pallas kernels for 0%

commit v1 on v0

--- a/solution.py
+++ b/solution.py
@@ -5,6 +5,12 @@
 
 D = 1024
 EPS = 1e-05
+
+
+def add_all(block, axis):
+    parts = lax.all_gather(block, axis, axis=0, tiled=False)
+    total = parts.sum(axis=0)
+    return total
 
 
 def lagged(values, shift_by):
@@ -60,7 +66,7 @@
 
 
 def summed_all(partial_sum):
-    return lax.psum(partial_sum, ("row", "col"))
+    return add_all(partial_sum, ("row", "col"))
 
 
 def token_stat(values):

time: 1180 us -> 1870 us (1.58)
  waiting for transfers between devices: 783 us -> 1400 us
  other arithmetic: 67.4 us -> 152 us
    all_gather x0 -> x2, waiting for transfers between devices: none -> 932 us  [add_all(): parts = lax.all_gather(block, axis, axis=0, tiled=False)]
    psum x2 -> x0, waiting for transfers between devices: 288 us -> none  [summed_all(): return lax.psum(partial_sum, ('row', 'col'))]
    reduce_sum x0 -> x2, other arithmetic: none -> 85.4 us  [add_all(): total = parts.sum(axis=0)]
  transfers between devices with their start and end apart: 17 -> 17, of which waited for: 15 -> 14; matrix products, arithmetic and copies ran while one was open for 14% -> 11% of each run, Pallas kernels for 0% -> 0%
where the time goes in v1:
time: 1870 us
  waiting for transfers between devices  1400 us (75%)
  other arithmetic  152 us (8%)
  matrix products  133 us (7%)
  blocking collectives  91.1 us (5%)
  local copies, waits for them, and re-layouts  38.1 us (2%)
  starting transfers between devices  35 us (2%)
    all_gather x2, waiting for transfers between devices, add_all(): parts = lax.all_gather(block, axis, axis=0, tiled=False)  932 us
    reduce_scatter x2, waiting for transfers between devices, own_share(): lax.psum_scatter(partial_sum, ('row', 'col'), scatter_dimension=1, tiled=...  197 us
    psum x1, waiting for transfers between devices, body(): lax.psum(grad_gate_w.astype(jnp.bfloat16), 'dp').astype(jnp.float32)  142 us
    reduce_sum x2, other arithmetic, add_all(): total = parts.sum(axis=0)  85.4 us
    all_gather x3, waiting for transfers between devices, full_width(): return lax.all_gather(part_half, ('row', 'col'), axis=1, tiled=True)  55 us
    psum x2, blocking collectives, token_stat(): return lax.psum(jnp.sum(values, axis=1), ('row', 'col'))  48.6 us
  transfers between devices with their start and end apart: 17, of which 14 were waited for; matrix products, arithmetic and copies ran while one was open for 11% of the time, Pallas kernels for 0%

profile of v1, /device:TPU:0, one launch (start us, length us, event | category | flops | bytes accessed | tf_op | source)
XLA Modules:
  0.0 1867.2 jit_solution(11339634559872991774)
XLA Ops:
  10.0 2.2 reduce
  13.1 4.2 all-to-all-start.1
  17.3 1.7 copy.81
  19.1 4.5 all-to-all-done.1
  23.6 3.6 all-to-all-start
  28.1 16.2 all-to-all-done
  45.1 22.4 %all-gather.8.cloned.1.call-done = bf16[3584,1024]{1,0:T(8,128)(2,1)} async-done(((bf16[3584,128]{1,0:T(8,128)(2,1)}), bf16[3584,1024]{1,0:T(8,128)(2,1)}) %all-gather.8.cloned.1.call-update) | async-done | bytes 7340048 | tf_op jit(solution)/shard_map/all_gather | solution.py:61
  67.5 4.7 fusion
  72.9 4.0 convolution_bitcast_fusion.1
  79.7 2.5 multiply_convert_fusion.7
  83.2 7.3 fusion.18
  93.1 3.6 all-to-all-start.2
  97.4 15.1 all-to-all-done.2
  112.4 30.8 %all_to_all.168 = bf16[512,2,576]{0,2,1:T(8,128)(2,1)S(1)} all-to-all(bf16[512,2,576]{0,2,1:T(8,128)(2,1)S(1)} %bitcast.167), channel_id=1, replica_groups=mesh['dp'=4,'row'=4,'col'=2] {'col'}, dimensions={1} | all-to-all | bytes 2359296 | tf_op jit(solution)/shard_map/all_to_all | solution.py:118
  143.3 3.6 all-to-all-start.4
  149.3 25.7 %all-to-all-done.4 = bf16[512,2,576]{0,2,1:T(8,128)(2,1)S(1)} async-done(((bf16[512,2,576]{0,2,1:T(8,128)(2,1)}), bf16[512,2,576]{0,2,1:T(8,128)(2,1)S(1)}, u32[]{:S(2)}, u32[]{:S(2)}) %all-to-all-start.4) | async-done | bytes 1179680 | tf_op jit(solution)/shard_map/all_to_all | solution.py:119
  175.3 455.0 %all-gather.14.cloned.1.call-done = f32[28672,1024]{1,0:T(8,128)} async-done(((f32[3584,1024]{1,0:T(8,128)}), f32[28672,1024]{1,0:T(8,128)}) %all-gather.14.cloned.1.call-update) | async-done | bytes 117440528 | tf_op jit(solution)/shard_map/all_gather | solution.py:11
  630.2 43.7 %reduce_sum.100 = f32[3584,1024]{1,0:T(8,128)} reduce(f32[8,3584,1024]{2,1,0:T(8,128)} %bitcast.17, f32[]{:T(128)} %constant.11.clone.1), dimensions={0}, to_apply=%region_1.2 | reduce | flops 25690112 | bytes 132120576 | tf_op jit(solution)/shard_map/reduce_sum | solution.py:12
  674.0 12.6 multiply_reduce_fusion
  686.6 9.4 multiply_convert_fusion
  696.1 9.9 fusion.19
  706.0 6.7 fusion.20
  712.7 17.4 multiply_convert_fusion.1
  730.1 7.8 fusion.22
  737.9 11.9 convolution_add_fusion
  750.6 101.5 %reduce-scatter.3.cloned.1.call-done = f32[3584,128]{1,0:T(8,128)} async-done(((f32[3584,1024]{1,0:T(8,128)}), f32[3584,128]{1,0:T(8,128)}) %reduce-scatter.3.cloned.1.call-update) | async-done | bytes 1835024 | tf_op jit(solution)/shard_map/reduce_scatter | solution.py:65
  852.2 4.2 multiply_reduce_fusion.1
  856.4 23.8 %psum.70 = f32[3584]{0:T(1024)S(1)} all-reduce(f32[3584]{0:T(1024)S(1)} %get-tuple-element.51), channel_id=1, replica_groups=mesh['dp'=4,'row'=4,'col'=2] {'row','col'}, use_global_device_ids=true, to_apply=%region_6.7 | all-reduce | flops 3584 | bytes 28672 | tf_op jit(solution)/shard_map/psum | solution.py:73
  880.2 4.0 fusion.16
  884.2 8.8 convolution_convert_fusion.1
  894.1 3.8 all-to-all-start.7
  897.9 8.8 convolution_convert_fusion
  907.9 32.6 %all-gather.12.cloned.1.call-done = bf16[3584,1024]{1,0:T(8,128)(2,1)} async-done(((bf16[3584,128]{1,0:T(8,128)(2,1)}), bf16[3584,1024]{1,0:T(8,128)(2,1)}) %all-gather.12.cloned.1.call-update) | async-done | bytes 7340048 | tf_op jit(solution)/shard_map/all_gather | solution.py:61
  940.5 7.8 multiply_reduce_fusion.5
  948.2 1.9 multiply_reduce_fusion.4
  951.7 2.0 multiply_convert_fusion.6
  953.7 4.6 all-to-all-start.8
  958.3 5.2 fusion.13
  964.0 2.3 reduce.1
  967.1 2.7 multiply_convert_fusion.4
  969.8 4.3 all-to-all-done.8
  974.1 3.7 all-to-all-start.6
  977.8 6.9 fusion.10
  984.7 1.4 copy.92
  986.2 3.6 all-to-all-start.5
  989.8 8.8 convolution_convert_fusion.2
  999.6 3.5 all-to-all-done.5
  1003.2 3.6 all-to-all-start.9
  1009.7 1.8 copy.93
  1011.6 3.1 all_to_all.146
  1014.7 6.0 all-to-all-done.9
  1022.4 10.6 convolution_bitcast_fusion
  1034.2 11.3 fusion.21
  1046.7 142.1 %all-reduce.10.cloned.1.call-done = (bf16[512,1152]{0,1:T(8,128)(2,1)}, bf16[512,1152]{0,1:T(8,128)(2,1)}, bf16[3,512,256]{2,1,0:T(8,128)(2,1)}, bf16[256,512]{1,0:T(8,128)(2,1)}, bf16[1152,512]{1,0:T(8,128)(2,1)}) async-done(((bf16[512,1152]{0,1:T(8,128)(2,1)}, bf16[512,1152]{0,1:T(8,128)(2,1)}, bf16[3,512,256]{2,1,0:T(8,128)(2,1)}, bf16[256,512]{1,0:T(8,128)(2,1)}, bf16[1152,512]{1,0:T(8,128)(2,1)}), ...) | async-done | bytes 4587536 | tf_op jit(solution)/shard_map/psum | solution.py:242
  1188.8 3.1 convert_element_type.173
  1191.9 1.7 copy.100
  1193.7 1.7 copy.99
  1197.5 95.9 %reduce-scatter.5.cloned.1.call-done = f32[3584,128]{1,0:T(8,128)} async-done(((f32[3584,1024]{1,0:T(8,128)}), f32[3584,128]{1,0:T(8,128)}) %reduce-scatter.5.cloned.1.call-update) | async-done | bytes 1835024 | tf_op jit(solution)/shard_map/reduce_scatter | solution.py:65
  1293.5 3.3 multiply_reduce_fusion.2
  1296.8 11.7 all-reduce.6
  1310.1 24.8 %psum.71 = f32[3584]{0:T(1024)S(1)} all-reduce(f32[3584]{0:T(1024)S(1)} %get-tuple-element.53), channel_id=1, replica_groups=mesh['dp'=4,'row'=4,'col'=2] {'row','col'}, use_global_device_ids=true, to_apply=%region_9.10 | all-reduce | flops 3584 | bytes 28672 | tf_op jit(solution)/shard_map/psum | solution.py:73
  1334.9 476.8 %all-gather.16.cloned.1.call-done = f32[28672,1024]{1,0:T(8,128)} async-done(((f32[3584,1024]{1,0:T(8,128)}), f32[28672,1024]{1,0:T(8,128)}) %all-gather.16.cloned.1.call-update) | async-done | bytes 117440528 | tf_op jit(solution)/shard_map/all_gather | solution.py:11
  1811.7 41.7 %reduce_sum.102 = f32[3584,1024]{1,0:T(8,128)} reduce(f32[8,3584,1024]{2,1,0:T(8,128)} %bitcast.25, f32[]{:T(128)} %constant.11.clone.1), dimensions={0}, to_apply=%region_3.4 | reduce | flops 25690112 | bytes 132120576 | tf_op jit(solution)/shard_map/reduce_sum | solution.py:12
  1853.4 6.7 multiply_add_fusion
  (185 shorter events, 33.4 us)
Async XLA Ops:
  7.2 60.3 %all-gather.8.cloned.1.call-start = ((), (), s32[]{:S(2)}) async-start(), calls=%async_computation.12 | async-start | bytes 8257536 | tf_op jit(solution)/shard_map/all_gather | solution.py:61
  7.2 10.1 copy-start.30
  10.0 9.1 copy-start.60
  13.1 10.5 all-to-all-start.1
  17.3 10.1 copy-start.43
  19.1 60.0 %copy-start.46 = (f32[128]{0:T(128)}, f32[128]{0:T(128)S(1)}, u32[]{:S(2)}) copy-start(f32[128]{0:T(128)S(1)} %get-tuple-element.87) | copy-start | bytes 1540
  19.1 60.0 %copy-start.48 = (f32[128]{0:T(128)}, f32[128]{0:T(128)S(1)}, u32[]{:S(2)}) copy-start(f32[128]{0:T(128)S(1)} %get-tuple-element.88) | copy-start | bytes 1540
  19.1 60.0 %copy-start.50 = (f32[128]{0:T(128)}, f32[128]{0:T(128)S(1)}, u32[]{:S(2)}) copy-start(f32[128]{0:T(128)S(1)} %get-tuple-element.89) | copy-start | bytes 1540
  23.6 20.7 %all-to-all-start = ((bf16[3,512,256]{1,0,2:T(4,128)(2,1)}), bf16[3,512,256]{1,0,2:T(4,128)(2,1)S(1)}, u32[]{:S(2)}, u32[]{:S(2)}) async-start(bf16[3,512,256]{1,0,2:T(4,128)(2,1)} %copy.81), calls=%async_computation | async-start | bytes 2097152 | tf_op jit(solution)/shard_map/all_to_all | solution.py:110
  27.2 603.0 %all-gather.14.cloned.1.call-start = ((), (), s32[]{:S(2)}) async-start(), calls=%async_computation.17 | async-start | bytes 132120576 | tf_op jit(solution)/shard_map/all_gather | solution.py:11
  27.5 51.6 %copy-start.39 = (f32[2,1792]{1,0:T(2,128)}, f32[2,1792]{1,0:T(2,128)S(1)}, u32[]{:S(2)}) copy-start(f32[2,1792]{1,0:T(2,128)S(1)} %get-tuple-element.85) | copy-start | bytes 43012
  27.6 51.6 %copy-start.41 = (f32[2,1792]{1,0:T(2,128)}, f32[2,1792]{1,0:T(2,128)S(1)}, u32[]{:S(2)}) copy-start(f32[2,1792]{1,0:T(2,128)S(1)} %get-tuple-element.86) | copy-start | bytes 43012
  28.1 54.2 %copy-start.20 = (bf16[1,2,512,128]{3,2,1,0:T(8,128)(2,1)}, bf16[1,2,512,128]{3,2,1,0:T(8,128)(2,1)S(1)}, u32[]{:S(2)}) copy-start(bf16[1,2,512,128]{3,2,1,0:T(8,128)(2,1)S(1)} %copy.85) | copy-start | bytes 786436
  45.1 27.2 %copy-start.19 = (bf16[3,512,2,128]{3,1,2,0:T(8,128)(2,1)}, bf16[3,512,2,128]{3,1,2,0:T(8,128)(2,1)S(1)}, u32[]{:S(2)}) copy-start(bf16[3,512,2,128]{3,1,2,0:T(8,128)(2,1)S(1)} %copy.82) | copy-start | bytes 2359300
  45.1 27.8 %copy-start.61 = (f32[1024]{0:T(1024)S(1)}, f32[1024]{0:T(1024)}, u32[]{:S(2)}) copy-start(f32[1024]{0:T(1024)} %param.20) | copy-start | bytes 12292
  67.5 5.4 copy-start.2
  77.3 1.8 copy-start.8
  77.3 2.4 copy-start.5
  79.1 3.1 copy-start
  90.5 622.2 %all-gather.10.cloned.1.call-start = ((), (), s32[]{:S(2)}) async-start(), calls=%async_computation.13 | async-start | bytes 8257536 | tf_op jit(solution)/shard_map/all_gather | solution.py:61
  91.7 5.0 copy-start.25
  93.1 19.3 %all-to-all-start.2 = ((bf16[512,2,576]{0,2,1:T(8,128)(2,1)}), bf16[512,2,576]{0,2,1:T(8,128)(2,1)S(1)}, u32[]{:S(2)}, u32[]{:S(2)}) async-start(bf16[512,2,576]{0,2,1:T(8,128)(2,1)} %bitcast.18), calls=%async_computation.2 | async-start | bytes 2359296 | tf_op jit(solution)/shard_map/all_to_all | solution.py:117
  143.3 31.8 %all-to-all-start.4 = ((bf16[512,2,576]{0,2,1:T(8,128)(2,1)}), bf16[512,2,576]{0,2,1:T(8,128)(2,1)S(1)}, u32[]{:S(2)}, u32[]{:S(2)}) async-start(bf16[512,2,576]{0,2,1:T(8,128)(2,1)} %bitcast.187), calls=%async_computation.4 | async-start | bytes 2359296 | tf_op jit(solution)/shard_map/all_to_all | solution.py:119
  146.9 705.3 %reduce-scatter.3.cloned.1.call-start = ((), (), s32[]{:S(2)}) async-start(), calls=%async_computation.14 | async-start | bytes 16515072 | tf_op jit(solution)/shard_map/reduce_scatter | solution.py:65
  175.2 537.5 %copy-start.26 = (bf16[2,72,8,512]{3,2,0,1:T(8,128)(2,1)}, bf16[2,72,8,512]{3,2,0,1:T(8,128)(2,1)S(1)}, u32[]{:S(2)}) copy-start(bf16[2,72,8,512]{3,2,0,1:T(8,128)(2,1)S(1)} %copy.109) | copy-start | bytes 3538948
  674.0 12.6 copy-start.53
  686.6 9.5 copy-start.28
  696.1 9.9 copy-start.12
  696.1 9.9 copy-start.29
  749.8 190.6 %all-gather.12.cloned.1.call-start = ((), (), s32[]{:S(2)}) async-start(), calls=%async_computation.15 | async-start | bytes 8257536 | tf_op jit(solution)/shard_map/all_gather | solution.py:61
  750.6 129.6 %copy-start.44 = (f32[128]{0:T(128)}, f32[128]{0:T(128)S(1)}, u32[]{:S(2)}) copy-start(f32[128]{0:T(128)S(1)} %dynamic_slice.14) | copy-start | bytes 1540
  750.6 129.6 %copy-start.11 = (bf16[2,1792,128]{2,1,0:T(8,128)(2,1)S(1)}, bf16[2,1792,128]{2,1,0:T(8,128)(2,1)}, u32[]{:S(2)}) copy-start(bf16[2,1792,128]{2,1,0:T(8,128)(2,1)} %param.13) | copy-start | bytes 2752516
  852.2 28.1 %copy-start.3 = (f32[3584,128]{1,0:T(8,128)S(1)}, f32[3584,128]{1,0:T(8,128)}, u32[]{:S(2)}) copy-start(f32[3584,128]{1,0:T(8,128)} %reduce-scatter.3.cloned.1.call-done) | copy-start | bytes 5505028
  880.2 4.0 copy-start.37
  894.1 59.6 %all-to-all-start.7 = ((bf16[2,512,576]{1,2,0:T(8,128)(2,1)}), bf16[2,512,576]{1,2,0:T(8,128)(2,1)S(1)}, u32[]{:S(2)}, u32[]{:S(2)}) async-start(bf16[2,512,576]{1,2,0:T(8,128)(2,1)} %bitcast.143), calls=%async_computation.9 | async-start | bytes 2359296 | tf_op jit(solution)/shard_map/all_to_all | solution.py:171
  906.7 33.8 %copy-start.1 = (f32[2,1792,128]{2,1,0:T(8,128)S(1)}, f32[2,1792,128]{2,1,0:T(8,128)}, u32[]{:S(2)}) copy-start(f32[2,1792,128]{2,1,0:T(8,128)} %copy-done) | copy-start | bytes 5505028
  906.7 33.8 %copy-start.21 = (bf16[1,2,512,128]{3,2,1,0:T(8,128)(2,1)S(1)}, bf16[1,2,512,128]{3,2,1,0:T(8,128)(2,1)}, u32[]{:S(2)}) copy-start(bf16[1,2,512,128]{3,2,1,0:T(8,128)(2,1)} %copy-done.20) | copy-start | bytes 786436
  940.4 7.8 copy-start.40
  940.5 7.8 copy-start.42
  953.7 4.6 copy-start.16
  953.7 9.8 copy-start.13
  953.7 20.4 %all-to-all-start.8 = ((bf16[2,512,576]{1,2,0:T(8,128)(2,1)}), bf16[2,512,576]{1,2,0:T(8,128)(2,1)}, u32[]{:S(2)}, u32[]{:S(2)}) async-start(bf16[2,512,576]{1,2,0:T(8,128)(2,1)} %bitcast.142), calls=%async_computation.10 | async-start | bytes 2359296 | tf_op jit(solution)/shard_map/all_to_all | solution.py:174
  963.6 3.5 copy-start.7
  967.1 10.7 copy-start.17
  967.1 10.7 copy-start.34
  967.1 10.7 copy-start.62
  974.1 12.0 all-to-all-start.6
  986.2 17.0 all-to-all-start.5
  1003.2 17.6 all-to-all-start.9
  1006.8 182.0 %all-reduce.10.cloned.1.call-start = ((), (), s32[]{:S(2)}) async-start(), calls=%async_computation.19 | async-start | bytes 9175040 | tf_op jit(solution)/shard_map/psum | solution.py:242
  1021.8 271.7 %reduce-scatter.5.cloned.1.call-start = ((), (), s32[]{:S(2)}) async-start(), calls=%async_computation.16 | async-start | bytes 16515072 | tf_op jit(solution)/shard_map/reduce_scatter | solution.py:65
  1033.0 778.7 %all-gather.16.cloned.1.call-start = ((), (), s32[]{:S(2)}) async-start(), calls=%async_computation.18 | async-start | bytes 132120576 | tf_op jit(solution)/shard_map/all_gather | solution.py:11
  1188.8 3.1 copy-start.23
  1193.6 1.8 copy-start.31
  1195.4 98.1 %copy-start.10 = (bf16[2,1792,128]{2,1,0:T(8,128)(2,1)S(1)}, bf16[2,1792,128]{2,1,0:T(8,128)(2,1)}, u32[]{:S(2)}) copy-start(bf16[2,1792,128]{2,1,0:T(8,128)(2,1)} %param.11) | copy-start | bytes 2752516
  1195.4 98.1 %copy-start.35 = (f32[3584]{0:T(1024)S(1)}, f32[3584]{0:T(1024)}, u32[]{:S(2)}) copy-start(f32[3584]{0:T(1024)} %copy-done.33) | copy-start | bytes 43012
  1195.4 98.1 %copy-start.55 = (f32[128]{0:T(128)S(1)}, f32[128]{0:T(128)}, u32[]{:S(2)}) copy-start(f32[128]{0:T(128)} %dynamic_slice.15) | copy-start | bytes 1540
  1196.7 100.1 %copy-start.52 = (bf16[3,128]{1,0:T(4,128)(2,1)S(1)}, bf16[3,128]{1,0:T(4,128)(2,1)}, u32[]{:S(2)}) copy-start(bf16[3,128]{1,0:T(4,128)(2,1)} %pad_maximum_fusion.3) | copy-start | bytes 2308
  1196.7 100.1 %copy-start.59 = (bf16[128]{0:T(256)(128)(2,1)S(1)}, bf16[128]{0:T(256)(128)(2,1)}, u32[]{:S(2)}) copy-start(bf16[128]{0:T(256)(128)(2,1)} %get-tuple-element.50) | copy-start | bytes 772
  1811.7 41.7 %copy-start.4 = (f32[3584,128]{1,0:T(8,128)S(1)}, f32[3584,128]{1,0:T(8,128)}, u32[]{:S(2)}) copy-start(f32[3584,128]{1,0:T(8,128)} %reduce-scatter.3.cloned.1.call-done) | copy-start | bytes 5505028
  1811.7 41.7 %copy-start.36 = (f32[3584]{0:T(1024)S(1)}, f32[3584]{0:T(1024)}, u32[]{:S(2)}) copy-start(f32[3584]{0:T(1024)} %copy-done.33) | copy-start | bytes 43012
  1811.7 41.7 %copy-start.38 = (f32[3584]{0:T(1024)S(1)}, f32[3584]{0:T(1024)}, u32[]{:S(2)}) copy-start(f32[3584]{0:T(1024)} %copy-done.37) | copy-start | bytes 43012
  1811.7 41.7 %copy-start.45 = (f32[128]{0:T(128)S(1)}, f32[128]{0:T(128)}, u32[]{:S(2)}) copy-start(f32[128]{0:T(128)} %copy-done.44) | copy-start | bytes 1540
  1811.7 41.7 %copy-start.56 = (f32[128]{0:T(128)S(1)}, f32[128]{0:T(128)}, u32[]{:S(2)}) copy-start(f32[128]{0:T(128)} %dynamic_slice.15) | copy-start | bytes 1540
  (16 other events, 18.9 us)
Sparse Core Ops, SparseCore 0:
  9.9 57.6 all-gather.7
  90.6 539.6 all-gather.13
  632.1 51.2 all-gather.9
  749.9 102.1 reduce-scatter.2
  884.4 56.0 all-gather.11
  1021.9 166.8 all-reduce.9
  1192.3 101.1 reduce-scatter.4
  1295.4 516.2 all-gather.15
